TPU v7x, 256 devices: a whole 4x4x8 slice. The times are simulated.
256 devices in a mesh: rep: 32 (over z, y), tp: 8 (over x, core).
Axes of the slice: x: 4, y: 4, z: 8, core: 2. Of those that a mesh axis runs over, the one named last changes fastest.
Arguments:
- image_grads: bfloat16 [512, 48, 1280], P('rep', 'tp'), may hold values from -6 to 6
- dest_rank: int32 [512], P('rep'), may hold values from 0 to 31, as said below
- dest_slot: int32 [512], P('rep'), may hold values from 0 to 31, as said below
- saved_inputs: bfloat16 [1024, 48, 1280], P('rep'), may hold values from -6 to 6
- up_weight: bfloat16 [1280, 5120], P(None, 'tp'), may hold values from -0.15625 to 0.15625
- down_weight: bfloat16 [5120, 1280], P('tp'), may hold values from -0.078125 to 0.078125
- norm_gain: float32 [1280], replicated, may hold values from 0.25 to 1.75
Outputs:
- input_grads: bfloat16 [1024, 48, 1280], P('rep', 'tp')
- up_grads: float32 [1280, 5120], P('rep', 'tp')
- down_grads: float32 [5120, 1280], P('tp', 'rep')
- gain_grads: float32 [1280], replicated
Inputs may be any that keep to these rules, and one draw needn't show every extreme that they name: `dest_rank`: the images of one index of rep go to different owners; each owner receives at most 32 images, and some owner receives exactly 32 in every draw. `dest_slot`: the images that one owner receives have distinct slots 0, 1, ... up to their count less one; other slots hold no image.
All inputs are finite; a program needn't handle non-finite values.
Results may differ from a plain program's by a relative error of at most 0.015.
Values may be sent and summed in bfloat16 or wider, within the bound.
A program may use at most 128 MiB of HBM per device.

v0:
```python
import jax
import jax.numpy as jnp
from jax import lax
from jax.sharding import Mesh
from jax.sharding import PartitionSpec as P

REP = ("rep_0", "rep_1")
epsilon = 1e-05
gelu_c = 0.7978845608028654
gelu_a = 0.044715


def scatter_axes(value, axes, dim):
    if not axes:
        return value
    nearer = lax.psum_scatter(value, axes[0], scatter_dimension=dim, tiled=True)
    return scatter_axes(nearer, axes[1:], dim)


def sent_to_all(value, axis):
    copies = jnp.broadcast_to(value, (lax.axis_size(axis), *value.shape))
    return lax.all_to_all(copies, axis, split_axis=0, concat_axis=0, tiled=True)


def of_everyone(value, axis):
    everything = sent_to_all(value, axis)
    return jnp.sum(everything, axis=0)


def gelu_value(preact):
    inner = jnp.tanh(gelu_c * (preact + gelu_a * preact**3))
    return 0.5 * preact * (1.0 + inner)


def gelu_slope(preact):
    inner = jnp.tanh(gelu_c * (preact + gelu_a * preact**3))
    return 0.5 * (1.0 + inner) + 0.5 * preact * (1.0 - inner * inner) * gelu_c * (
        1.0 + 3.0 * gelu_a * preact * preact
    )


def outbound(images, dest_rank, dest_slot, groups, capacity):
    rank_ids = jnp.arange(groups, dtype=jnp.int32)
    one_hot = dest_rank[None, :] == rank_ids[:, None]
    packed = jnp.einsum(
        "ek,kpd->epd", one_hot.astype(jnp.bfloat16), images, preferred_element_type=jnp.float32
    ).astype(jnp.bfloat16)
    present = jnp.any(one_hot, axis=1)
    slot_sent = jnp.sum(jnp.where(one_hot, dest_slot[None, :], 0), axis=1) + jnp.where(
        present, 0, capacity
    )
    return (packed, slot_sent)


def compact(inbound, slot_recv, capacity):
    slot_ids = jnp.arange(capacity, dtype=jnp.int32)
    picker = (slot_recv[None, :] == slot_ids[:, None]).astype(jnp.bfloat16)
    return jnp.einsum("ce,epd->cpd", picker, inbound, preferred_element_type=jnp.float32).astype(
        jnp.bfloat16
    )


def local(image_grads, dest_rank, dest_slot, saved_inputs, up_weight, down_weight, norm_gain):
    groups = lax.axis_size(REP)
    capacity = saved_inputs.shape[0]
    patches = saved_inputs.shape[1]
    width = saved_inputs.shape[2]
    slab = image_grads.shape[1]
    packed, slot_sent = outbound(image_grads, dest_rank, dest_slot, groups, capacity)
    inbound, slot_recv = (
        lax.all_to_all(packed, REP, split_axis=0, concat_axis=0, tiled=True),
        lax.all_to_all(slot_sent, REP, split_axis=0, concat_axis=0, tiled=True),
    )
    routed = lax.all_gather(compact(inbound, slot_recv, capacity), "tp", axis=1, tiled=True)
    rows = capacity * patches
    grads = routed.reshape(rows, width)
    values = saved_inputs.reshape(rows, width).astype(jnp.float32)
    mean_v = jnp.mean(values, axis=1, keepdims=True)
    var_v = jnp.mean((values - mean_v) ** 2, axis=1, keepdims=True)
    inv_std = 1.0 / jnp.sqrt(var_v + epsilon)
    centred = (values - mean_v) * inv_std
    normed = (centred * norm_gain[None, :]).astype(jnp.bfloat16)
    preact = jnp.dot(normed, up_weight, preferred_element_type=jnp.float32)
    hidden = gelu_value(preact).astype(jnp.bfloat16)
    grad_hidden = jnp.dot(grads, down_weight.T, preferred_element_type=jnp.float32)
    grad_pre = (grad_hidden * gelu_slope(preact)).astype(jnp.bfloat16)
    down_local = jnp.dot(hidden.T, grads, preferred_element_type=jnp.float32)
    up_local = jnp.dot(normed.T, grad_pre, preferred_element_type=jnp.float32)
    partial_normed = jnp.dot(grad_pre, up_weight.T, preferred_element_type=jnp.float32)
    up_grads, down_grads = (
        scatter_axes(up_local.astype(jnp.bfloat16), REP, 0).astype(jnp.float32),
        scatter_axes(down_local.astype(jnp.bfloat16), REP, 1).astype(jnp.float32),
    )
    start = lax.axis_index("tp") * slab
    grad_normed = lax.psum(partial_normed.astype(jnp.bfloat16), "tp").astype(jnp.float32)
    gain_grads = of_everyone(jnp.sum(grad_normed * centred, axis=0), REP)
    scaled = grad_normed * norm_gain[None, :]
    first = jnp.mean(scaled, axis=1, keepdims=True)
    second = jnp.mean(scaled * centred, axis=1, keepdims=True)
    result = grads.astype(jnp.float32) + inv_std * (scaled - first - centred * second)
    result = result.reshape(capacity, patches, width)
    input_grads = lax.dynamic_slice_in_dim(result, start, slab, 1).astype(jnp.bfloat16)
    return (input_grads, up_grads, down_grads, gain_grads)


def solution(mesh):
    split = Mesh(mesh.devices.reshape(8, 4, mesh.shape["tp"]), ("rep_0", "rep_1", "tp"))
    return jax.shard_map(
        local,
        mesh=split,
        in_specs=(
            P(REP, "tp", None),
            P(REP),
            P(REP),
            P(REP, None, None),
            P(None, "tp"),
            P("tp", None),
            P(),
        ),
        out_specs=(P(REP, "tp", None), P(REP, "tp"), P("tp", REP), P()),
        check_vma=False,
    )
```

profile of v0, /device:TPU:2, one launch (start us, length us, event | category | flops | bytes accessed | tf_op | source)
XLA Modules:
  0.0 318.9 jit_solution(2042661000471552826)
XLA Ops:
  7.2 0.9 fusion.27
  8.0 0.8 select_reduce_fusion
  8.8 0.7 copy.29
  9.5 11.5 %all-to-all-start = ((s32[32,1,1]{2,1,0:T(1,128)}), s32[32,1,1]{2,1,0:T(1,128)S(1)}, u32[]{:S(2)}, u32[]{:S(2)}) async-start(s32[32,1,1]{2,1,0:T(1,128)} %copy.29), calls=%async_computation | async-start | bytes 32768 | tf_op jit(solution)/shard_map/all_to_all | solution.py:72
  21.0 1.4 convolution_convert_fusion.4
  22.4 1.1 copy.30
  23.5 7.2 %all-to-all-done = s32[32,1,1]{2,1,0:T(1,128)S(1)} async-done(((s32[32,1,1]{2,1,0:T(1,128)}), s32[32,1,1]{2,1,0:T(1,128)S(1)}, u32[]{:S(2)}, u32[]{:S(2)}) %all-to-all-start) | async-done | bytes 160 | tf_op jit(solution)/shard_map/all_to_all | solution.py:72
  30.7 3.9 %all-to-all-start.1 = ((bf16[32,6,1280]{2,1,0:T(8,128)(2,1)}), bf16[32,6,1280]{2,1,0:T(8,128)(2,1)S(1)}, u32[]{:S(2)}, u32[]{:S(2)}) async-start(bf16[32,6,1280]{2,1,0:T(8,128)(2,1)} %copy.30), calls=%async_computation.1 | async-start | bytes 1310720 | tf_op jit(solution)/shard_map/all_to_all | solution.py:71
  34.6 0.0 all-gather.2.cloned.1.call-start
  34.6 0.7 reduce.3
  35.3 18.5 %all-to-all-done.1 = bf16[32,6,1280]{2,1,0:T(8,128)(2,1)S(1)} async-done(((bf16[32,6,1280]{2,1,0:T(8,128)(2,1)}), bf16[32,6,1280]{2,1,0:T(8,128)(2,1)S(1)}, u32[]{:S(2)}, u32[]{:S(2)}) %all-to-all-start.1) | async-done | bytes 491552 | tf_op jit(solution)/shard_map/all_to_all | solution.py:71
  53.8 1.1 convolution_convert_fusion.3
  54.8 0.0 all-gather.2.cloned.1.call-update
  54.9 0.2 reduce-scatter.11.cloned.1.call-start
  55.1 2.7 convert_reduce_fusion
  57.8 0.1 div.18
  57.9 3.3 %multiply_reduce_fusion = f32[32,48]{1,0:T(8,128)S(1)} fusion(bf16[32,48,1280]{2,1,0:T(8,128)(2,1)} %param.10, f32[32,48]{1,0:T(8,128)S(1)} %broadcast_multiply_fusion), kind=kLoop, calls=%fused_computation.13 | loop fusion | flops 7862784 | bytes 3944448 | tf_op jit(solution)/shard_map/reduce_sum | solution.py:79
  61.2 0.1 sqrt.6
  61.3 3.0 multiply_convert_fusion
  64.3 2.0 copy-done.2
  66.3 5.2 %fusion.34 = f32[1536,640]{1,0:T(8,128)} fusion(bf16[1536,1280]{1,0:T(8,128)(2,1)S(1)} %multiply_convert_fusion, bf16[1280,640]{1,0:T(8,128)(2,1)S(1)} %copy-done), kind=kOutput, calls=%fused_computation.56 | convolution fusion | flops 2516582400 | bytes 9502720 | tf_op jit(solution)/shard_map/dot_general | solution.py:83
  71.5 12.3 %all-gather.2.cloned.1.call-done = bf16[32,48,1280]{2,0,1:T(8,128)(2,1)} async-done(((bf16[32,6,1280]{2,0,1:T(8,128)(2,1)}), bf16[32,48,1280]{2,0,1:T(8,128)(2,1)}) %all-gather.2.cloned.1.call-update) | async-done | bytes 3932176 | tf_op jit(solution)/shard_map/all_gather | solution.py:74
  83.8 4.4 %copy.32 = bf16[32,48,1280]{2,1,0:T(8,128)(2,1)S(1)} copy(bf16[32,48,1280]{2,0,1:T(8,128)(2,1)} %all-gather.2.cloned.1.call-done) | data formatting | bytes 7864320 | tf_op jit(solution)/shard_map/all_gather | solution.py:74
  88.2 1.9 copy-done.1
  90.1 5.1 %convolution_convert_fusion.1 = bf16[640,1280]{0,1:T(8,128)(2,1)} fusion(bf16[1536,1280]{1,0:T(8,128)(2,1)S(1)} %bitcast.34, f32[1536,640]{1,0:T(8,128)S(1)} %copy-done.5), kind=kOutput, calls=%fused_computation.28 | convolution fusion | flops 2526248960 | bytes 9502720 | tf_op jit(solution)/shard_map/dot_general | solution.py:87
  95.2 0.3 all-reduce.4.cloned.1.call-start
  95.5 8.2 %fusion.17 = bf16[1536,640]{1,0:T(8,128)(2,1)S(1)} fusion(f32[1536,640]{1,0:T(8,128)} %fusion.34, bf16[1536,1280]{1,0:T(8,128)(2,1)} %bitcast.35, bf16[640,1280]{1,0:T(8,128)(2,1)S(1)} %copy-done.4), kind=kOutput, calls=%fused_computation.26 | convolution fusion | flops 2535260160 | bytes 11468800 | tf_op jit(solution)/shard_map/dot_general | solution.py:85
  103.7 1.3 copy-done.6
  104.9 4.7 %convolution_convert_fusion = bf16[1536,1280]{1,0:T(8,128)(2,1)} fusion(bf16[1536,640]{1,0:T(8,128)(2,1)S(1)} %fusion.17, bf16[1280,640]{1,0:T(8,128)(2,1)S(1)} %copy-done), kind=kOutput, calls=%fused_computation.14 | convolution fusion | flops 2518548480 | bytes 7536640 | tf_op jit(solution)/shard_map/dot_general | solution.py:89
  109.7 0.0 all-reduce.4.cloned.1.call-update
  109.7 0.0 reduce-scatter.9.cloned.1.call-start
  109.7 7.2 %convolution_convert_fusion.2 = bf16[1280,640]{1,0:T(8,128)(2,1)} fusion(bf16[1536,1280]{1,0:T(8,128)(2,1)} %copy-done.2, bf16[1536,640]{1,0:T(8,128)(2,1)} %copy-done.6), kind=kOutput, calls=%fused_computation.29 | convolution fusion | flops 2517401600 | bytes 7536640 | tf_op jit(solution)/shard_map/dot_general | solution.py:88
  116.9 0.0 reduce-scatter.15.cloned.1.call-start
  117.0 20.4 %reduce-scatter.11.cloned.1.call-done = bf16[640,160]{0,1:T(8,128)(2,1)} async-done(((bf16[640,1280]{0,1:T(8,128)(2,1)}), bf16[640,160]{0,1:T(8,128)(2,1)}) %reduce-scatter.11.cloned.1.call-update) | async-done | bytes 204816 | tf_op jit(solution)/shard_map/reduce_scatter | solution.py:16
  137.4 74.8 %all-reduce.4.cloned.1.call-done = bf16[1536,1280]{1,0:T(8,128)(2,1)} async-done(((bf16[1536,1280]{1,0:T(8,128)(2,1)}), bf16[1536,1280]{1,0:T(8,128)(2,1)}) %all-reduce.4.cloned.1.call-update) | async-done | bytes 3932176 | tf_op jit(solution)/shard_map/psum | solution.py:95
  212.2 5.8 %fusion.7 = (f32[1280]{0:T(1024)S(1)}, f32[1536]{0:T(1024)S(1)}, f32[1536]{0:T(1024)S(1)}) fusion(bf16[1536,1280]{1,0:T(8,128)(2,1)} %all-reduce.4.cloned.1.call-done, bf16[32,48,1280]{2,1,0:T(8,128)(2,1)} %param.10, f32[1536]{0:T(1024)S(1)} %div.18, f32[1536]{0:T(1024)S(1)} %sqrt.6, f32[1280]{0:T(1024)S(1)} %copy-done.3), kind=kLoop, calls=%fused_computation.9 | loop fusion | flops 19656448 | bytes 7899136 | tf_op jit(solution)/shard_map/reduce_sum | solution.py:96
  218.0 0.7 broadcast_in_dim.38
  218.8 9.9 %all-to-all-start.2 = ((f32[32,1,1280]{2,1,0:T(1,128)}), f32[32,1,1280]{2,1,0:T(1,128)S(1)}, u32[]{:S(2)}, u32[]{:S(2)}) async-start(f32[32,1,1280]{2,1,0:T(1,128)} %broadcast_in_dim.38), calls=%async_computation.4 | async-start | bytes 327680 | tf_op jit(solution)/shard_map/all_to_all | solution.py:22
  228.6 0.0 reduce-scatter.13.cloned.1.call-start
  228.7 31.9 %reduce-scatter.9.cloned.1.call-done = bf16[160,640]{1,0:T(8,128)(2,1)} async-done(((bf16[1280,640]{1,0:T(8,128)(2,1)}), bf16[160,640]{1,0:T(8,128)(2,1)}) %reduce-scatter.9.cloned.1.call-update) | async-done | bytes 204816 | tf_op jit(solution)/shard_map/reduce_scatter | solution.py:16
  260.6 6.1 %fusion.5 = bf16[1536,1280]{1,0:T(8,128)(2,1)S(1)} fusion(bf16[1536,1280]{1,0:T(8,128)(2,1)} %all-reduce.4.cloned.1.call-done, bf16[32,48,1280]{2,1,0:T(8,128)(2,1)} %param.10, f32[1536]{0:T(1024)S(1)} %get-tuple-element.7, f32[1536]{0:T(1024)S(1)} %get-tuple-element.8, f32[1280]{0:T(1024)S(1)} %copy-done.3, f32[1536]{0:T(1024)S(1)} %div.18, ...), kind=kLoop, calls=%fused_computation.7 | loop fusion | flops 23592960 | bytes 15758336 | tf_op jit(solution)/shard_map/add | solution.py:100
  266.7 0.2 constant_dynamic-slice_fusion
  266.9 0.9 copy.40
  267.8 0.7 reduce_sum.69
  268.5 16.8 %reduce-scatter.15.cloned.1.call-done = bf16[640,40]{0,1:T(8,128)(2,1)} async-done(((bf16[640,160]{0,1:T(8,128)(2,1)}), bf16[640,40]{0,1:T(8,128)(2,1)}) %reduce-scatter.15.cloned.1.call-update) | async-done | bytes 51216
  285.3 1.5 convert_element_type.66
  286.8 23.8 %reduce-scatter.13.cloned.1.call-done = bf16[40,640]{1,0:T(8,128)(2,1)} async-done(((bf16[160,640]{1,0:T(8,128)(2,1)}), bf16[40,640]{1,0:T(8,128)(2,1)}) %reduce-scatter.13.cloned.1.call-update) | async-done | bytes 51216
  310.6 1.5 convert_element_type.63
  (20 shorter events, 0.1 us)
Async XLA Ops:
  7.2 59.1 %copy-start = (bf16[1280,640]{1,0:T(8,128)(2,1)S(1)}, bf16[1280,640]{1,0:T(8,128)(2,1)}, u32[]{:S(2)}) copy-start(bf16[1280,640]{1,0:T(8,128)(2,1)} %param.11) | copy-start | bytes 4915204
  9.5 21.2 %all-to-all-start = ((s32[32,1,1]{2,1,0:T(1,128)}), s32[32,1,1]{2,1,0:T(1,128)S(1)}, u32[]{:S(2)}, u32[]{:S(2)}) async-start(s32[32,1,1]{2,1,0:T(1,128)} %copy.29), calls=%async_computation | async-start | bytes 32768 | tf_op jit(solution)/shard_map/all_to_all | solution.py:72
  30.7 23.1 %all-to-all-start.1 = ((bf16[32,6,1280]{2,1,0:T(8,128)(2,1)}), bf16[32,6,1280]{2,1,0:T(8,128)(2,1)S(1)}, u32[]{:S(2)}, u32[]{:S(2)}) async-start(bf16[32,6,1280]{2,1,0:T(8,128)(2,1)} %copy.30), calls=%async_computation.1 | async-start | bytes 1310720 | tf_op jit(solution)/shard_map/all_to_all | solution.py:71
  34.6 49.2 %all-gather.2.cloned.1.call-start = ((), (), s32[]{:S(2)}) async-start(), calls=%async_computation.7 | async-start | bytes 4423680 | tf_op jit(solution)/shard_map/all_gather | solution.py:74
  54.8 6.4 %copy-start.3 = (f32[1280]{0:T(1024)S(1)}, f32[1280]{0:T(1024)}, u32[]{:S(2)}) copy-start(f32[1280]{0:T(1024)} %param.13) | copy-start | bytes 15364
  54.9 82.5 %reduce-scatter.11.cloned.1.call-start = ((), (), s32[]{:S(2)}) async-start(), calls=%async_computation.10 | async-start | bytes 1843200 | tf_op jit(solution)/shard_map/reduce_scatter | solution.py:16
  64.3 2.0 copy-start.2
  83.8 6.3 %copy-start.5 = (f32[1536,640]{1,0:T(8,128)S(1)}, f32[1536,640]{1,0:T(8,128)}, u32[]{:S(2)}) copy-start(f32[1536,640]{1,0:T(8,128)} %fusion.34) | copy-start | bytes 11796484
  88.2 1.9 copy-start.1
  90.1 5.4 %copy-start.4 = (bf16[640,1280]{1,0:T(8,128)(2,1)S(1)}, bf16[640,1280]{1,0:T(8,128)(2,1)}, u32[]{:S(2)}) copy-start(bf16[640,1280]{1,0:T(8,128)(2,1)} %param.12) | copy-start | bytes 4915204
  95.2 117.0 %all-reduce.4.cloned.1.call-start = ((), (), s32[]{:S(2)}) async-start(), calls=%async_computation.8 | async-start | bytes 7864320 | tf_op jit(solution)/shard_map/psum | solution.py:95
  103.7 1.3 copy-start.6
  109.7 150.9 %reduce-scatter.9.cloned.1.call-start = ((), (), s32[]{:S(2)}) async-start(), calls=%async_computation.9 | async-start | bytes 1843200 | tf_op jit(solution)/shard_map/reduce_scatter | solution.py:16
  116.9 168.4 %reduce-scatter.15.cloned.1.call-start = ((), (), s32[]{:S(2)}) async-start(), calls=%async_computation.12 | async-start | bytes 256000
  218.8 49.0 %all-to-all-start.2 = ((f32[32,1,1280]{2,1,0:T(1,128)}), f32[32,1,1280]{2,1,0:T(1,128)S(1)}, u32[]{:S(2)}, u32[]{:S(2)}) async-start(f32[32,1,1280]{2,1,0:T(1,128)} %broadcast_in_dim.38), calls=%async_computation.4 | async-start | bytes 327680 | tf_op jit(solution)/shard_map/all_to_all | solution.py:22
  228.6 82.0 %reduce-scatter.13.cloned.1.call-start = ((), (), s32[]{:S(2)}) async-start(), calls=%async_computation.11 | async-start | bytes 256000
Sparse Core Ops, SparseCore 0:
  55.0 28.8 all-gather.1
  95.3 41.9 reduce-scatter.10
  139.7 72.4 all-reduce.3
  214.6 45.9 reduce-scatter.8
  263.0 22.2 reduce-scatter.14
  287.7 22.8 reduce-scatter.12
where the time goes:
time: 319 us
  waiting for transfers between devices  206 us (65%)
  matrix products  32.8 us (10%)
  other arithmetic  26.8 us (8%)
  starting transfers between devices  25.9 us (8%)
  between operations  14.3 us (4%)
  local copies, waits for them, and re-layouts  13.3 us (4%)
    psum x1, waiting for transfers between devices, local(): lax.psum(partial_normed.astype(jnp.bfloat16), 'tp').astype(jnp.float32)  74.8 us
    reduce_scatter x2, waiting for transfers between devices, scatter_axes(): nearer = lax.psum_scatter(value, axes[0], scatter_dimension=dim, tiled=True)  52.3 us
    unnamed x8, waiting for transfers between devices  40.7 us
    all_to_all x1, waiting for transfers between devices, local(): lax.all_to_all(packed, REP, split_axis=0, concat_axis=0, tiled=True)  18.5 us
    all_gather x1, waiting for transfers between devices, local(): lax.all_gather(compact(inbound, slot_recv, capacity), 'tp', axis=1, tiled...  12.3 us
    all_to_all x1, starting transfers between devices, local(): lax.all_to_all(slot_sent, REP, split_axis=0, concat_axis=0, tiled=True)  11.5 us
    all_to_all x1, starting transfers between devices, sent_to_all(): return lax.all_to_all(copies, axis, split_axis=0, concat_axis=0, tiled=True)  9.85 us
    dot_general x1, matrix products, local(): jnp.dot(grads, down_weight.T, preferred_element_type=jnp.float32)  8.16 us
  transfers between devices with their start and end apart: 9, of which 8 were waited for; matrix products, arithmetic and copies ran while one was open for 17% of the time, Pallas kernels for 0%

commit v1 on v0

--- a/solution.py
+++ b/solution.py
@@ -8,6 +8,11 @@
 epsilon = 1e-05
 gelu_c = 0.7978845608028654
 gelu_a = 0.044715
+
+
+def tiled_gather(x, axis, dim):
+    copies = jnp.concatenate([x] * lax.axis_size(axis), axis=dim)
+    return lax.all_to_all(copies, axis, dim, dim, tiled=True)
 
 
 def scatter_axes(value, axes, dim):
@@ -71,7 +76,7 @@
         lax.all_to_all(packed, REP, split_axis=0, concat_axis=0, tiled=True),
         lax.all_to_all(slot_sent, REP, split_axis=0, concat_axis=0, tiled=True),
     )
-    routed = lax.all_gather(compact(inbound, slot_recv, capacity), "tp", axis=1, tiled=True)
+    routed = tiled_gather(compact(inbound, slot_recv, capacity), "tp", 1)
     rows = capacity * patches
     grads = routed.reshape(rows, width)
     values = saved_inputs.reshape(rows, width).astype(jnp.float32)

time: 319 us -> 261 us (0.82)
  waiting for transfers between devices: 206 us -> 136 us
  local copies, waits for them, and re-layouts: 13.3 us -> 19.1 us
  starting transfers between devices: 25.9 us -> 30.3 us
    reduce_scatter x2, waiting for transfers between devices: 52.3 us -> 14.5 us  [scatter_axes(): nearer = lax.psum_scatter(value, axes[0], scatter_dimension=dim, tiled=True)]
    all_to_all x0 -> x1, waiting for transfers between devices: none -> 29.2 us  [tiled_gather(): return lax.all_to_all(copies, axis, dim, dim, tiled=True)]
    psum x1, waiting for transfers between devices: 74.8 us -> 48.3 us  [local(): lax.psum(partial_normed.astype(jnp.bfloat16), 'tp').astype(jnp.float32)]
    unnamed x8 -> x7, waiting for transfers between devices: 40.7 us -> 15.6 us
    all_gather x1 -> x0, waiting for transfers between devices: 12.3 us -> none  [local(): lax.all_gather(compact(inbound, slot_recv, capacity), 'tp', axis=1, tiled...]
    unnamed x15 -> x21, local copies, waits for them, and re-layouts: 5.99 us -> 11 us
    all_to_all x0 -> x1, starting transfers between devices: none -> 4.93 us  [tiled_gather(): return lax.all_to_all(copies, axis, dim, dim, tiled=True)]
    all_to_all x0 -> x1, local copies, waits for them, and re-layouts: none -> 4.42 us  [tiled_gather(): return lax.all_to_all(copies, axis, dim, dim, tiled=True)]
  transfers between devices with their start and end apart: 9 -> 9, of which waited for: 8 -> 7; matrix products, arithmetic and copies ran while one was open for 17% -> 20% of each run, Pallas kernels for 0% -> 0%
where the time goes in v1:
time: 261 us
  waiting for transfers between devices  136 us (52%)
  matrix products  32.8 us (13%)
  starting transfers between devices  30.3 us (12%)
  other arithmetic  26.8 us (10%)
  local copies, waits for them, and re-layouts  19.1 us (7%)
  between operations  15.4 us (6%)
    psum x1, waiting for transfers between devices, local(): lax.psum(partial_normed.astype(jnp.bfloat16), 'tp').astype(jnp.float32)  48.3 us
    all_to_all x1, waiting for transfers between devices, tiled_gather(): return lax.all_to_all(copies, axis, dim, dim, tiled=True)  29.2 us
    all_to_all x1, waiting for transfers between devices, local(): lax.all_to_all(packed, REP, split_axis=0, concat_axis=0, tiled=True)  18.5 us
    unnamed x7, waiting for transfers between devices  15.6 us
    reduce_scatter x2, waiting for transfers between devices, scatter_axes(): nearer = lax.psum_scatter(value, axes[0], scatter_dimension=dim, tiled=True)  14.5 us
    all_to_all x1, starting transfers between devices, local(): lax.all_to_all(slot_sent, REP, split_axis=0, concat_axis=0, tiled=True)  11.5 us
    unnamed x21, local copies, waits for them, and re-layouts  11 us
    all_to_all x1, starting transfers between devices, sent_to_all(): return lax.all_to_all(copies, axis, split_axis=0, concat_axis=0, tiled=True)  9.58 us
  transfers between devices with their start and end apart: 9, of which 7 were waited for; matrix products, arithmetic and copies ran while one was open for 20% of the time, Pallas kernels for 0%

profile of v1, /device:TPU:2, one launch (start us, length us, event | category | flops | bytes accessed | tf_op | source)
XLA Modules:
  0.0 260.8 jit_solution(8158484133178665468)
XLA Ops:
  8.0 0.9 fusion.27
  8.9 0.8 select_reduce_fusion
  9.6 0.7 copy.29
  10.3 11.5 %all-to-all-start = ((s32[32,1,1]{2,1,0:T(1,128)}), s32[32,1,1]{2,1,0:T(1,128)S(1)}, u32[]{:S(2)}, u32[]{:S(2)}) async-start(s32[32,1,1]{2,1,0:T(1,128)} %copy.29), calls=%async_computation | async-start | bytes 32768 | tf_op jit(solution)/shard_map/all_to_all | solution.py:77
  21.8 1.4 convolution_convert_fusion.4
  23.2 1.1 copy.30
  24.3 7.2 %all-to-all-done = s32[32,1,1]{2,1,0:T(1,128)S(1)} async-done(((s32[32,1,1]{2,1,0:T(1,128)}), s32[32,1,1]{2,1,0:T(1,128)S(1)}, u32[]{:S(2)}, u32[]{:S(2)}) %all-to-all-start) | async-done | bytes 160 | tf_op jit(solution)/shard_map/all_to_all | solution.py:77
  31.5 3.9 %all-to-all-start.1 = ((bf16[32,6,1280]{2,1,0:T(8,128)(2,1)}), bf16[32,6,1280]{2,1,0:T(8,128)(2,1)S(1)}, u32[]{:S(2)}, u32[]{:S(2)}) async-start(bf16[32,6,1280]{2,1,0:T(8,128)(2,1)} %copy.30), calls=%async_computation.1 | async-start | bytes 1310720 | tf_op jit(solution)/shard_map/all_to_all | solution.py:76
  35.4 0.7 reduce.3
  36.1 18.5 %all-to-all-done.1 = bf16[32,6,1280]{2,1,0:T(8,128)(2,1)S(1)} async-done(((bf16[32,6,1280]{2,1,0:T(8,128)(2,1)}), bf16[32,6,1280]{2,1,0:T(8,128)(2,1)S(1)}, u32[]{:S(2)}, u32[]{:S(2)}) %all-to-all-start.1) | async-done | bytes 491552 | tf_op jit(solution)/shard_map/all_to_all | solution.py:76
  54.6 1.1 constant_dynamic-update-slice_fusion.7
  55.7 0.8 constant_dynamic-update-slice_fusion.6
  56.5 0.8 constant_dynamic-update-slice_fusion.5
  57.3 0.8 constant_dynamic-update-slice_fusion.4
  58.2 0.8 constant_dynamic-update-slice_fusion.3
  59.0 0.8 constant_dynamic-update-slice_fusion.2
  59.8 0.8 constant_dynamic-update-slice_fusion.1
  60.6 0.8 constant_dynamic-update-slice_fusion
  61.5 4.9 %all-to-all-start.2 = ((bf16[32,48,1280]{2,0,1:T(8,128)(2,1)}), bf16[32,48,1280]{2,0,1:T(8,128)(2,1)}, u32[]{:S(2)}, u32[]{:S(2)}) async-start(bf16[32,48,1280]{2,0,1:T(8,128)(2,1)} %constant_dynamic-update-slice_fusion), calls=%async_computation.2 | async-start | bytes 7864320 | tf_op jit(solution)/shard_map/all_to_all | solution.py:15
  66.4 2.7 %convert_reduce_fusion = f32[32,48]{1,0:T(8,128)S(1)} fusion(bf16[32,48,1280]{2,1,0:T(8,128)(2,1)} %param.10), kind=kLoop, calls=%fused_computation.17 | loop fusion | flops 3930624 | bytes 3938304 | tf_op jit(solution)/shard_map/reduce_sum | solution.py:83
  69.1 0.1 div.18
  69.2 3.3 %multiply_reduce_fusion = f32[32,48]{1,0:T(8,128)S(1)} fusion(bf16[32,48,1280]{2,1,0:T(8,128)(2,1)} %param.10, f32[32,48]{1,0:T(8,128)S(1)} %broadcast_multiply_fusion), kind=kLoop, calls=%fused_computation.13 | loop fusion | flops 7862784 | bytes 3944448 | tf_op jit(solution)/shard_map/reduce_sum | solution.py:84
  72.6 2.9 %multiply_convert_fusion = bf16[1536,1280]{1,0:T(8,128)(2,1)S(1)} fusion(bf16[32,48,1280]{2,1,0:T(8,128)(2,1)} %param.10, f32[1280]{0:T(1024)S(1)} %copy-done.3, f32[1536]{0:T(1024)S(1)} %div.18, f32[1536]{0:T(1024)S(1)} %sqrt.6), kind=kLoop, calls=%fused_computation.12 | loop fusion | flops 9830400 | bytes 7881728 | tf_op jit(solution)/shard_map/convert_element_type | solution.py:87
  75.5 2.0 copy-done.2
  77.5 5.2 %fusion.34 = f32[1536,640]{1,0:T(8,128)} fusion(bf16[1536,1280]{1,0:T(8,128)(2,1)S(1)} %multiply_convert_fusion, bf16[1280,640]{1,0:T(8,128)(2,1)S(1)} %copy-done), kind=kOutput, calls=%fused_computation.64 | convolution fusion | flops 2516582400 | bytes 9502720 | tf_op jit(solution)/shard_map/dot_general | solution.py:88
  82.7 29.2 %all-to-all-done.2 = bf16[32,48,1280]{2,0,1:T(8,128)(2,1)} async-done(((bf16[32,48,1280]{2,0,1:T(8,128)(2,1)}), bf16[32,48,1280]{2,0,1:T(8,128)(2,1)}, u32[]{:S(2)}, u32[]{:S(2)}) %all-to-all-start.2) | async-done | bytes 3932192 | tf_op jit(solution)/shard_map/all_to_all | solution.py:15
  111.9 4.4 %copy.32 = bf16[32,48,1280]{2,1,0:T(8,128)(2,1)S(1)} copy(bf16[32,48,1280]{2,0,1:T(8,128)(2,1)} %all-to-all-done.2) | data formatting | bytes 7864320 | tf_op jit(solution)/shard_map/all_to_all | solution.py:15
  116.3 1.9 copy-done.1
  118.2 5.1 %convolution_convert_fusion.1 = bf16[640,1280]{0,1:T(8,128)(2,1)} fusion(bf16[1536,1280]{1,0:T(8,128)(2,1)S(1)} %bitcast.36, f32[1536,640]{1,0:T(8,128)S(1)} %copy-done.5), kind=kOutput, calls=%fused_computation.28 | convolution fusion | flops 2526248960 | bytes 9502720 | tf_op jit(solution)/shard_map/dot_general | solution.py:92
  123.3 0.3 all-reduce.4.cloned.1.call-start
  123.6 8.2 %fusion.17 = bf16[1536,640]{1,0:T(8,128)(2,1)S(1)} fusion(f32[1536,640]{1,0:T(8,128)} %fusion.34, bf16[1536,1280]{1,0:T(8,128)(2,1)} %bitcast.37, bf16[640,1280]{1,0:T(8,128)(2,1)S(1)} %copy-done.4), kind=kOutput, calls=%fused_computation.26 | convolution fusion | flops 2535260160 | bytes 11468800 | tf_op jit(solution)/shard_map/dot_general | solution.py:90
  131.8 1.3 copy-done.6
  133.0 4.7 %convolution_convert_fusion = bf16[1536,1280]{1,0:T(8,128)(2,1)} fusion(bf16[1536,640]{1,0:T(8,128)(2,1)S(1)} %fusion.17, bf16[1280,640]{1,0:T(8,128)(2,1)S(1)} %copy-done), kind=kOutput, calls=%fused_computation.14 | convolution fusion | flops 2518548480 | bytes 7536640 | tf_op jit(solution)/shard_map/dot_general | solution.py:94
  137.8 7.2 %convolution_convert_fusion.2 = bf16[1280,640]{1,0:T(8,128)(2,1)} fusion(bf16[1536,1280]{1,0:T(8,128)(2,1)} %copy-done.2, bf16[1536,640]{1,0:T(8,128)(2,1)} %copy-done.6), kind=kOutput, calls=%fused_computation.29 | convolution fusion | flops 2517401600 | bytes 7536640 | tf_op jit(solution)/shard_map/dot_general | solution.py:93
  145.1 14.5 %reduce-scatter.11.cloned.1.call-done = bf16[640,160]{0,1:T(8,128)(2,1)} async-done(((bf16[640,1280]{0,1:T(8,128)(2,1)}), bf16[640,160]{0,1:T(8,128)(2,1)}) %reduce-scatter.11.cloned.1.call-update) | async-done | bytes 204816 | tf_op jit(solution)/shard_map/reduce_scatter | solution.py:21
  159.7 48.3 %all-reduce.4.cloned.1.call-done = bf16[1536,1280]{1,0:T(8,128)(2,1)} async-done(((bf16[1536,1280]{1,0:T(8,128)(2,1)}), bf16[1536,1280]{1,0:T(8,128)(2,1)}) %all-reduce.4.cloned.1.call-update) | async-done | bytes 3932176 | tf_op jit(solution)/shard_map/psum | solution.py:100
  208.0 5.8 %fusion.7 = (f32[1280]{0:T(1024)S(1)}, f32[1536]{0:T(1024)S(1)}, f32[1536]{0:T(1024)S(1)}) fusion(bf16[1536,1280]{1,0:T(8,128)(2,1)} %all-reduce.4.cloned.1.call-done, bf16[32,48,1280]{2,1,0:T(8,128)(2,1)} %param.10, f32[1536]{0:T(1024)S(1)} %div.18, f32[1536]{0:T(1024)S(1)} %sqrt.6, f32[1280]{0:T(1024)S(1)} %copy-done.3), kind=kLoop, calls=%fused_computation.9 | loop fusion | flops 19656448 | bytes 7899136 | tf_op jit(solution)/shard_map/reduce_sum | solution.py:101
  213.8 0.7 broadcast_in_dim.38
  214.5 9.6 %all-to-all-start.3 = ((f32[32,1,1280]{2,1,0:T(1,128)}), f32[32,1,1280]{2,1,0:T(1,128)S(1)}, u32[]{:S(2)}, u32[]{:S(2)}) async-start(f32[32,1,1280]{2,1,0:T(1,128)} %broadcast_in_dim.38), calls=%async_computation.5 | async-start | bytes 327680 | tf_op jit(solution)/shard_map/all_to_all | solution.py:27
  224.2 0.5 reduce-scatter.13.cloned.1.call-update
  224.7 6.1 %fusion.5 = bf16[1536,1280]{1,0:T(8,128)(2,1)S(1)} fusion(bf16[1536,1280]{1,0:T(8,128)(2,1)} %all-reduce.4.cloned.1.call-done, bf16[32,48,1280]{2,1,0:T(8,128)(2,1)} %param.10, f32[1536]{0:T(1024)S(1)} %get-tuple-element.9, f32[1536]{0:T(1024)S(1)} %get-tuple-element.10, f32[1280]{0:T(1024)S(1)} %copy-done.3, f32[1536]{0:T(1024)S(1)} %div.18, ...), kind=kLoop, calls=%fused_computation.7 | loop fusion | flops 23592960 | bytes 15758336 | tf_op jit(solution)/shard_map/add | solution.py:105
  230.8 0.2 constant_dynamic-slice_fusion
  231.0 0.9 copy.40
  231.9 3.1 %all-to-all-done.3 = f32[32,1,1280]{2,1,0:T(1,128)S(1)} async-done(((f32[32,1,1280]{2,1,0:T(1,128)}), f32[32,1,1280]{2,1,0:T(1,128)S(1)}, u32[]{:S(2)}, u32[]{:S(2)}) %all-to-all-start.3) | async-done | bytes 163872 | tf_op jit(solution)/shard_map/all_to_all | solution.py:27
  235.0 0.7 reduce_sum.69
  235.7 1.5 convert_element_type.66
  237.1 15.1 %reduce-scatter.13.cloned.1.call-done = bf16[40,640]{1,0:T(8,128)(2,1)} async-done(((bf16[160,640]{1,0:T(8,128)(2,1)}), bf16[40,640]{1,0:T(8,128)(2,1)}) %reduce-scatter.13.cloned.1.call-update) | async-done | bytes 51216
  252.2 1.5 convert_element_type.63
  (26 shorter events, 0.3 us)
Async XLA Ops:
  8.0 69.5 %copy-start = (bf16[1280,640]{1,0:T(8,128)(2,1)S(1)}, bf16[1280,640]{1,0:T(8,128)(2,1)}, u32[]{:S(2)}) copy-start(bf16[1280,640]{1,0:T(8,128)(2,1)} %param.11) | copy-start | bytes 4915204
  10.3 21.2 %all-to-all-start = ((s32[32,1,1]{2,1,0:T(1,128)}), s32[32,1,1]{2,1,0:T(1,128)S(1)}, u32[]{:S(2)}, u32[]{:S(2)}) async-start(s32[32,1,1]{2,1,0:T(1,128)} %copy.29), calls=%async_computation | async-start | bytes 32768 | tf_op jit(solution)/shard_map/all_to_all | solution.py:77
  31.5 23.1 %all-to-all-start.1 = ((bf16[32,6,1280]{2,1,0:T(8,128)(2,1)}), bf16[32,6,1280]{2,1,0:T(8,128)(2,1)S(1)}, u32[]{:S(2)}, u32[]{:S(2)}) async-start(bf16[32,6,1280]{2,1,0:T(8,128)(2,1)} %copy.30), calls=%async_computation.1 | async-start | bytes 1310720 | tf_op jit(solution)/shard_map/all_to_all | solution.py:76
  61.5 50.4 %all-to-all-start.2 = ((bf16[32,48,1280]{2,0,1:T(8,128)(2,1)}), bf16[32,48,1280]{2,0,1:T(8,128)(2,1)}, u32[]{:S(2)}, u32[]{:S(2)}) async-start(bf16[32,48,1280]{2,0,1:T(8,128)(2,1)} %constant_dynamic-update-slice_fusion), calls=%async_computation.2 | async-start | bytes 7864320 | tf_op jit(solution)/shard_map/all_to_all | solution.py:15
  66.4 6.2 %copy-start.3 = (f32[1280]{0:T(1024)S(1)}, f32[1280]{0:T(1024)}, u32[]{:S(2)}) copy-start(f32[1280]{0:T(1024)} %param.13) | copy-start | bytes 15364
  66.4 93.2 %reduce-scatter.11.cloned.1.call-start = ((), (), s32[]{:S(2)}) async-start(), calls=%async_computation.10 | async-start | bytes 1843200 | tf_op jit(solution)/shard_map/reduce_scatter | solution.py:21
  75.5 2.0 copy-start.2
  111.9 6.3 %copy-start.5 = (f32[1536,640]{1,0:T(8,128)S(1)}, f32[1536,640]{1,0:T(8,128)}, u32[]{:S(2)}) copy-start(f32[1536,640]{1,0:T(8,128)} %fusion.34) | copy-start | bytes 11796484
  116.3 1.9 copy-start.1
  118.2 5.4 %copy-start.4 = (bf16[640,1280]{1,0:T(8,128)(2,1)S(1)}, bf16[640,1280]{1,0:T(8,128)(2,1)}, u32[]{:S(2)}) copy-start(bf16[640,1280]{1,0:T(8,128)(2,1)} %param.12) | copy-start | bytes 4915204
  123.3 84.7 %all-reduce.4.cloned.1.call-start = ((), (), s32[]{:S(2)}) async-start(), calls=%async_computation.8 | async-start | bytes 7864320 | tf_op jit(solution)/shard_map/psum | solution.py:100
  131.8 1.3 copy-start.6
  137.8 86.4 %reduce-scatter.9.cloned.1.call-start = ((), (), s32[]{:S(2)}) async-start(), calls=%async_computation.9 | async-start | bytes 1843200 | tf_op jit(solution)/shard_map/reduce_scatter | solution.py:21
  145.1 90.6 %reduce-scatter.15.cloned.1.call-start = ((), (), s32[]{:S(2)}) async-start(), calls=%async_computation.12 | async-start | bytes 256000
  214.5 20.5 %all-to-all-start.3 = ((f32[32,1,1280]{2,1,0:T(1,128)}), f32[32,1,1280]{2,1,0:T(1,128)S(1)}, u32[]{:S(2)}, u32[]{:S(2)}) async-start(f32[32,1,1280]{2,1,0:T(1,128)} %broadcast_in_dim.38), calls=%async_computation.5 | async-start | bytes 327680 | tf_op jit(solution)/shard_map/all_to_all | solution.py:27
  224.1 28.1 %reduce-scatter.13.cloned.1.call-start = ((), (), s32[]{:S(2)}) async-start(), calls=%async_computation.11 | async-start | bytes 256000
Sparse Core Ops, SparseCore 0:
  123.4 36.1 reduce-scatter.10
  162.2 39.5 reduce-scatter.8
  204.4 21.6 reduce-scatter.14
  228.5 23.6 reduce-scatter.12
Sparse Core Ops, SparseCore 1:
  137.9 70.0 all-reduce.3
